TPU v7x, 32 devices: a whole 2x2x4 slice. The times are simulated.
32 devices in a mesh: chan: 8 (over y, x, core), tm: 4 (over z).
Axes of the slice: x: 2, y: 2, z: 4, core: 2. Of those that a mesh axis runs over, the one named last changes fastest.
Arguments:
- records: float32 [2560, 4, 7936], P('chan', 'tm'), may hold values from -6 to 6
- offsets: int32 [4], P('tm'), may hold values from 0 to 256
Outputs:
- correlations: float32 [2, 640, 2, 20480], P(None, 'tm', None, 'chan')
All inputs are finite; a program needn't handle non-finite values.
Results may differ from a plain program's by a relative error of at most 0.0001.
Values sent between devices are 32-bit elements; how exact they have to be, the bound alone decides.
A program may use at most 128 MiB of HBM per device.

v0:
```python
import functools
import math

import jax
import jax.numpy as jnp
import numpy as np
from jax import lax
from jax.experimental import pallas as pl
from jax.experimental.pallas import tpu as pltpu
from jax.sharding import PartitionSpec as P

SRC = 8
LEN = 7680
FB = 640
FLO = 64
SMOOTH = 64
ROUNDS = 2
M = 15
L = LEN // M
Q0 = FLO // M
NQ = 48
BASE = 16
START = BASE + M * Q0 - FLO
ROWS = START + M // 2 + M * (NQ - 1) + 5
LANES = 128
PARTS = LEN // LANES


def split(x):
    hi = x.astype(jnp.bfloat16)
    return hi, (x - hi.astype(jnp.float32)).astype(jnp.bfloat16)


def tables():
    a = np.arange(L)
    q = Q0 + np.arange(NQ)
    angle = 2.0 * math.pi * ((q[:, None] * a[None, :]) % L) / L
    full = np.concatenate([np.cos(angle), np.sin(angle)]).astype(np.float32)
    hi = full.astype(jnp.bfloat16)
    lo = (full - hi.astype(np.float32)).astype(jnp.bfloat16)
    both = np.concatenate([hi, lo])
    r = np.arange(1, M // 2 + 1)
    turn = 2.0 * math.pi * (r[:, None] * a[None, :]) / LEN
    twiddle = np.stack([np.cos(turn), np.sin(turn)], 1).reshape(2 * len(r), L)
    twiddle = np.repeat(twiddle[:, None, :], 8, 1).astype(np.float32)
    k = np.arange(FB)
    band = (np.abs(k[:, None] - k[None, :]) <= SMOOTH).astype(jnp.bfloat16)
    return both, twiddle, band


C3 = math.sqrt(3.0) / 2.0
C51, C52 = math.cos(2 * math.pi / 5), math.cos(4 * math.pi / 5)
S51, S52 = math.sin(2 * math.pi / 5), math.sin(4 * math.pi / 5)


def dft3(x0, x1, x2):
    t = x1 + x2
    return x0 + t, x0 - 0.5 * t, C3 * (x2 - x1)


def dft5(x):
    t1, t2 = x[1] + x[4], x[2] + x[3]
    d1, d2 = x[1] - x[4], x[2] - x[3]
    re0 = x[0] + t1 + t2
    re1 = x[0] + C51 * t1 + C52 * t2
    re2 = x[0] + C52 * t1 + C51 * t2
    im1 = -(S51 * d1 + S52 * d2)
    im2 = S51 * d2 - S52 * d1
    return re0, re1, im1, re2, im2


def dft15(x):
    columns = [dft3(*[x[(5 * n1 + 3 * n2) % 15] for n1 in range(3)]) for n2 in range(5)]
    z = dft5([c[0] for c in columns])
    u = dft5([c[1] for c in columns])
    v = dft5([c[2] for c in columns])
    out = {}
    out[(0, 0)] = (z[0], None)
    out[(0, 1)] = (z[1], z[2])
    out[(0, 2)] = (z[3], z[4])
    out[(1, 0)] = (u[0], v[0])
    for j, (b, s) in ((1, (1, 2)), (2, (3, 4))):
        out[(1, j)] = (u[b] - v[s], u[s] + v[b])
        out[(1, 5 - j)] = (u[b] + v[s], v[b] - u[s])
    bins = [None] * 8
    for (k1, k2), (re, im) in out.items():
        k = (10 * k1 + 6 * k2) % 15
        if k <= 7:
            bins[k] = (re, im)
        else:
            bins[15 - k] = (re, -im)
    return bins


def spectra(rows, off_ref, x_ref, both_ref, twiddle_ref, band_ref, o_ref, hi_ref, lo_ref, re_ref, im_ref):
    step = pl.program_id(0)
    off = off_ref[0]
    lane = lax.broadcasted_iota(jnp.int32, (16, LANES), 1)

    def put(row, c0, a0, value):
        hi, lo = split(value)
        hi_ref[pl.ds(row * LANES + c0, 16), pl.ds(a0, LANES)] = hi
        lo_ref[pl.ds(row * LANES + c0, 16), pl.ds(a0, LANES)] = lo

    extra = rows - PARTS

    def block(i, carry):
        c0 = pl.multiple_of(i * 16, 16)

        def load(j):
            return x_ref[pl.ds(c0 * rows + j, 16, stride=rows), :]

        for t in range(L // LANES):
            x = []
            for b in range(M):
                j = b * (L // LANES) + t
                value = load(j)
                if j < extra:
                    value = jnp.where(lane + j * LANES < off, load(j + PARTS), value)
                x.append(value)
            bins = dft15(x)
            a0 = t * LANES
            put(0, c0, a0, bins[0][0])
            for r in range(1, 8):
                re, im = bins[r]
                cos = twiddle_ref[2 * r - 2, :, a0 : a0 + LANES]
                sin = twiddle_ref[2 * r - 1, :, a0 : a0 + LANES]
                cos = jnp.concatenate([cos, cos], 0)
                sin = jnp.concatenate([sin, sin], 0)
                put(2 * r - 1, c0, a0, re * cos + im * sin)
                put(2 * r, c0, a0, im * cos - re * sin)
        return carry

    lax.fori_loop(0, LANES // 16, block, 0)

    nt = (((1,), (1,)), ((), ()))

    def second(row, count):
        window = slice(row * LANES, (row + count) * LANES)
        p = lax.dot_general(both_ref[...], hi_ref[window, :], nt, preferred_element_type=jnp.float32)
        s = lax.dot_general(both_ref[: 2 * NQ, :], lo_ref[window, :], nt, preferred_element_type=jnp.float32)
        return p[: 2 * NQ] + p[2 * NQ :] + s

    z = second(0, 1)
    re_ref[pl.ds(START, NQ, stride=M), :] = z[:NQ]
    im_ref[pl.ds(START, NQ, stride=M), :] = -z[NQ:]
    for r in range(1, 8):
        z = second(2 * r - 1, 2)
        rc, rs = z[:NQ, :LANES], z[NQ:, :LANES]
        ic, is_ = z[:NQ, LANES:], z[NQ:, LANES:]
        re_ref[pl.ds(START + r, NQ, stride=M), :] = rc + is_
        im_ref[pl.ds(START + r, NQ, stride=M), :] = ic - rs
        re_ref[pl.ds(START - r, NQ, stride=M), :] = rc - is_
        im_ref[pl.ds(START - r, NQ, stride=M), :] = -ic - rs
    re = re_ref[BASE : BASE + FB, :]
    im = im_ref[BASE : BASE + FB, :]
    hi, lo = split(jnp.sqrt(re * re + im * im))
    total = jnp.dot(band_ref[...], jnp.concatenate([hi, lo], 1), preferred_element_type=jnp.float32)
    k = lax.broadcasted_iota(jnp.int32, (FB, LANES), 0)
    count = jnp.minimum(k + SMOOTH, FB - 1) - jnp.maximum(k - SMOOTH, 0) + 1
    smooth = (total[:, :LANES] + total[:, LANES:]) / count.astype(jnp.float32)
    scale = 1.0 / (smooth + 1e-06)
    re, im = re * scale, im * scale
    whole = pl.num_programs(0) - 1

    @pl.when(step < whole)
    def _():
        o_ref[:, :LANES] = re
        o_ref[:, LANES:] = im

    @pl.when(step == whole)
    def _():
        low = lax.broadcasted_iota(jnp.int32, (FB, LANES), 1) < LANES // 2
        o_ref[:, :LANES] = jnp.where(low, re, pltpu.roll(im, LANES // 2, 1))


def whiten(records, offsets):
    chans = records.shape[0]
    rows = records.shape[2] // LANES
    flat = records.reshape(chans * rows, LANES)
    both, twiddle, band = tables()
    steps = -(-chans // LANES)
    keep = lambda shape: pl.BlockSpec(shape, lambda i: (0,) * len(shape))
    return pl.pallas_call(
        functools.partial(spectra, rows),
        grid=(steps,),
        in_specs=[
            pl.BlockSpec(memory_space=pltpu.SMEM),
            pl.BlockSpec((LANES * rows, LANES), lambda i: (i, 0)),
            keep(both.shape),
            keep(twiddle.shape),
            keep(band.shape),
        ],
        out_specs=pl.BlockSpec((FB, 2 * LANES), lambda i: (0, i)),
        out_shape=jax.ShapeDtypeStruct((FB, 2 * chans), jnp.float32),
        scratch_shapes=[
            pltpu.VMEM((M * LANES, L), jnp.bfloat16),
            pltpu.VMEM((M * LANES, L), jnp.bfloat16),
            pltpu.VMEM((ROWS + 8, LANES), jnp.float32),
            pltpu.VMEM((ROWS + 8, LANES), jnp.float32),
        ],
        compiler_params=pltpu.CompilerParams(vmem_limit_bytes=48 << 20),
        name="whiten",
    )(offsets, flat, jnp.asarray(both), jnp.asarray(twiddle), jnp.asarray(band))


KB = 8


def pairing(wins, chans, scale, a_ref, b_ref, e_ref, o_ref, x_ref):
    tiles = chans * SRC // LANES
    per = LANES // SRC
    full = chans // LANES
    for t in range(-(-chans // LANES)):
        if t < full:
            re = a_ref[:, :, 2 * t * LANES : (2 * t + 1) * LANES]
            im = a_ref[:, :, (2 * t + 1) * LANES : (2 * t + 2) * LANES]
            width = LANES * SRC
        else:
            re = a_ref[:, :, 2 * t * LANES : (2 * t + 1) * LANES]
            im = pltpu.roll(re, LANES // 2, 2)
            width = LANES * SRC // 2
        both = jnp.concatenate([re, im], 0).reshape(2 * wins * KB, LANES)
        hi, lo = split(both)
        lhs = jnp.concatenate([hi, lo], 1)
        x_ref[:, t * LANES * SRC : t * LANES * SRC + width] = jnp.dot(
            lhs, e_ref[:, :width], preferred_element_type=jnp.float32
        )
    for tile in range(tiles):
        lanes = slice(tile * LANES, (tile + 1) * LANES)
        ar = [x_ref[w * KB : (w + 1) * KB, lanes] for w in range(wins)]
        ai = [x_ref[(wins + w) * KB : (wins + w + 1) * KB, lanes] for w in range(wins)]
        for rnd in range(ROUNDS):
            real = imag = None
            for w in range(wins):
                br, bi = b_ref[rnd, w, 0], b_ref[rnd, w, 1]
                p = ar[w] * br + ai[w] * bi
                q = ai[w] * br - ar[w] * bi
                real = p if real is None else real + p
                imag = q if imag is None else imag + q
            o_ref[rnd, pl.ds(2 * tile, KB, stride=2 * tiles), :] = real * scale
            o_ref[rnd, pl.ds(2 * tile + 1, KB, stride=2 * tiles), :] = imag * scale


def correlate(grouped, sources):
    wins, bins, wide = grouped.shape
    chans = wide // 2
    tiles = chans * SRC // LANES
    spread = (np.arange(LANES)[:, None] == np.arange(LANES * SRC)[None, :] // SRC).astype(jnp.bfloat16)
    spread = np.concatenate([spread, spread])
    out = pl.pallas_call(
        functools.partial(pairing, wins, chans, 1.0 / wins),
        grid=(bins // KB,),
        in_specs=[
            pl.BlockSpec((wins, KB, wide), lambda i: (0, i, 0)),
            pl.BlockSpec((ROUNDS, wins, 2, KB, LANES), lambda i: (0, 0, 0, i, 0)),
            pl.BlockSpec(spread.shape, lambda i: (0, 0)),
        ],
        out_specs=pl.BlockSpec((ROUNDS, KB * tiles * 2, LANES), lambda i: (0, i, 0)),
        out_shape=jax.ShapeDtypeStruct((ROUNDS, bins * tiles * 2, LANES), jnp.float32),
        scratch_shapes=[pltpu.VMEM((2 * wins * KB, chans * SRC), jnp.float32)],
        compiler_params=pltpu.CompilerParams(vmem_limit_bytes=48 << 20),
        name="pairing",
    )(grouped, sources, jnp.asarray(spread))
    out = out.reshape(ROUNDS, bins, tiles, 2, LANES).transpose(0, 1, 3, 2, 4)
    return out.reshape(ROUNDS, bins, 2, tiles * LANES)


def passed_along(block, axis, distance):
    devices = range(lax.axis_size(axis))
    route = [((i - distance) % len(devices), i) for i in devices]
    return lax.ppermute(block, axis, route)


def shards(records, offsets):
    wins = records.shape[1]
    assert wins == 1
    white = whiten(records, offsets)
    n = lax.axis_size("tm")
    grouped = lax.all_to_all(white.reshape(n, FB // n, white.shape[1]), "tm", split_axis=0, concat_axis=0)
    own = jnp.stack([grouped[:, :, :SRC], grouped[:, :, LANES : LANES + SRC]], 1)
    shape = own.shape
    flat = own.reshape(-1, LANES)
    got = [passed_along(flat, "chan", -rnd).reshape(shape) for rnd in range(1, ROUNDS + 1)]
    sources = jnp.tile(jnp.stack(got), (1, 1, 1, 1, LANES // SRC))
    return correlate(grouped, sources)


def solution(mesh):
    return jax.shard_map(
        shards,
        mesh=mesh,
        in_specs=(P("chan", "tm", None), P("tm")),
        out_specs=P(None, "tm", None, "chan"),
        check_vma=False,
    )
```

profile of v0, /device:TPU:0, one launch (start us, length us, event | category | flops | bytes accessed | tf_op | source)
XLA Modules:
  0.0 110.2 jit_solution(8558634459770457016)
XLA Ops:
  0.7 0.0 copy-start
  0.7 1.1 %copy-done = bf16[640,640]{1,0:T(8,128)(2,1)S(1)} copy-done((bf16[640,640]{1,0:T(8,128)(2,1)S(1)}, bf16[640,640]{1,0:T(8,128)(2,1)}, u32[]{:S(2)}) %copy-start) | copy-done | bytes 819224
  1.8 0.0 copy-start.2
  1.8 0.9 copy-done.2
  2.7 0.0 copy-start.3
  2.7 0.9 copy-done.3
  3.7 14.4 %whiten.1 = f32[640,640]{1,0:T(8,128)S(1)} custom-call(s32[1]{0:T(128)S(6)} %copy.29.off_ref, f32[19840,128]{1,0:T(8,128)} %bitcast.19, bf16[192,512]{1,0:T(8,128)(2,1)S(1)} %copy-done.3, f32[14,8,512]{2,1,0:T(8,128)S(1)} %copy-done.2, bf16[640,640]{1,0:T(8,128)(2,1)S(1)} %copy-done), custom_call_target="tpu_custom_call" | custom-call | tf_op jit(solution)/shard_map/whiten/pallas_call | solution.py:184
  18.0 44.5 %all_to_all.5.a_ref = f32[4,160,640]{2,1,0:T(8,128)S(1)} all-to-all(f32[4,160,640]{2,1,0:T(8,128)S(1)} %bitcast.16), channel_id=1, replica_groups=mesh['chan'=8,'tm'=4] {'tm'}, dimensions={0} | all-to-all | bytes 3276800 | tf_op jit(solution)/shard_map/all_to_all | solution.py:280
  62.7 0.3 reshape.21
  63.0 1.1 %collective-permute-start = (f32[80,128]{1,0:T(8,128)S(1)}, f32[80,128]{1,0:T(8,128)S(1)}, u32[]{:S(2)}, u32[]{:S(2)}) collective-permute-start(f32[80,128]{1,0:T(8,128)S(1)} %reshape.21), channel_id=1, source_target_pairs={{4,0},{8,4},{12,8},{16,12},{20,16},{24,20},{28,24},{0,28},{5,1},{9... | collective-permute-start | bytes 122888 | tf_op jit(solution)/shard_map/ppermute | solution.py:272
  64.2 1.4 %collective-permute-start.1 = (f32[80,128]{1,0:T(8,128)S(1)}, f32[80,128]{1,0:T(8,128)S(1)}, u32[]{:S(2)}, u32[]{:S(2)}) collective-permute-start(f32[80,128]{1,0:T(8,128)S(1)} %reshape.21), channel_id=1, source_target_pairs={{8,0},{12,4},{16,8},{20,12},{24,16},{28,20},{0,24},{4,28},{9,1},{1... | collective-permute-start | bytes 122888 | tf_op jit(solution)/shard_map/ppermute | solution.py:272
  65.6 0.3 collective-permute-done
  65.8 0.4 stack_reshape.6
  66.2 0.3 copy.22
  66.5 1.7 %collective-permute-done.1 = f32[80,128]{1,0:T(8,128)S(1)} collective-permute-done((f32[80,128]{1,0:T(8,128)S(1)}, f32[80,128]{1,0:T(8,128)S(1)}, u32[]{:S(2)}, u32[]{:S(2)}) %collective-permute-start.1) | collective-permute-done | bytes 40992 | tf_op jit(solution)/shard_map/ppermute | solution.py:272
  68.2 0.4 stack_reshape.7
  68.5 0.3 copy.23
  68.9 1.5 %broadcast_bitcast_fusion = f32[2,4,2,160,128]{3,4,2,1,0:T(8,128)} fusion(f32[2,4,2,160,8]{3,4,2,1,0:T(8,128)S(1)} %pad_maximum_fusion.1), kind=kLoop, calls=%fused_computation.1 | loop fusion | bytes 1392640 | tf_op jit(solution)/shard_map/tile | solution.py:285
  70.3 2.0 %copy.24.b_ref = f32[2,4,2,160,128]{4,3,2,1,0:T(8,128)S(1)} copy(f32[2,4,2,160,128]{3,4,2,1,0:T(8,128)} %broadcast_bitcast_fusion) | data formatting | bytes 2621440 | tf_op jit(solution)/shard_map/tile | solution.py:285
  72.3 0.0 copy-done.1
  72.3 12.1 %pairing.1 = f32[2,6400,128]{2,1,0:T(8,128)} custom-call(f32[4,160,640]{2,1,0:T(8,128)S(1)} %all_to_all.5.a_ref, f32[2,4,2,160,128]{4,3,2,1,0:T(8,128)S(1)} %copy.24.b_ref, bf16[256,1024]{1,0:T(8,128)(2,1)S(1)} %copy-done.1), custom_call_target="tpu_custom_call" | custom-call | tf_op jit(solution)/shard_map/pairing/pallas_call | solution.py:251
  84.4 6.6 %copy.28 = f32[2,160,20,2,128]{4,2,1,3,0:T(8,128)} copy(f32[2,160,20,2,128]{4,3,2,1,0:T(2,128)} %bitcast.18) | data formatting | bytes 13107200 | tf_op jit(solution)/shard_map/reshape | solution.py:265
  91.0 8.5 %reshape.23 = f32[2,160,2,2560]{3,1,2,0:T(8,128)} reshape(f32[2,160,2,20,128]{4,3,1,2,0:T(8,128)} %bitcast.17) | data formatting | bytes 13107200 | tf_op jit(solution)/shard_map/reshape | solution.py:266
  99.5 10.7 %copy.26 = f32[2,160,2,2560]{3,2,1,0:T(2,128)} copy(f32[2,160,2,2560]{3,1,2,0:T(8,128)} %reshape.23) | data formatting | bytes 13107200 | tf_op jit(solution)/shard_map/reshape | solution.py:266
  (5 shorter events, 0.2 us)
Async XLA Ops:
  0.7 1.1 %copy-start = (bf16[640,640]{1,0:T(8,128)(2,1)S(1)}, bf16[640,640]{1,0:T(8,128)(2,1)}, u32[]{:S(2)}) copy-start(bf16[640,640]{1,0:T(8,128)(2,1)} %constant.10.clone.band_ref) | copy-start | bytes 2457604
  1.8 0.9 copy-start.2
  2.7 0.9 copy-start.3
  63.0 2.8 %collective-permute-start = (f32[80,128]{1,0:T(8,128)S(1)}, f32[80,128]{1,0:T(8,128)S(1)}, u32[]{:S(2)}, u32[]{:S(2)}) collective-permute-start(f32[80,128]{1,0:T(8,128)S(1)} %reshape.21), channel_id=1, source_target_pairs={{4,0},{8,4},{12,8},{16,12},{20,16},{24,20},{28,24},{0,28},{5,1},{9... | collective-permute-start | bytes 122888 | tf_op jit(solution)/shard_map/ppermute | solution.py:272
  64.2 4.0 %collective-permute-start.1 = (f32[80,128]{1,0:T(8,128)S(1)}, f32[80,128]{1,0:T(8,128)S(1)}, u32[]{:S(2)}, u32[]{:S(2)}) collective-permute-start(f32[80,128]{1,0:T(8,128)S(1)} %reshape.21), channel_id=1, source_target_pairs={{8,0},{12,4},{16,8},{20,12},{24,16},{28,20},{0,24},{4,28},{9,1},{1... | collective-permute-start | bytes 122888 | tf_op jit(solution)/shard_map/ppermute | solution.py:272
  70.3 2.0 %copy-start.1 = (bf16[256,1024]{1,0:T(8,128)(2,1)S(1)}, bf16[256,1024]{1,0:T(8,128)(2,1)}, u32[]{:S(2)}) copy-start(bf16[256,1024]{1,0:T(8,128)(2,1)} %constant.11.clone.e_ref) | copy-start | bytes 1572868
where the time goes:
time: 111 us; the launch traced here: 110 us
  blocking collectives  44.5 us (40%)
  local copies, waits for them, and re-layouts  34 us (31%)
  Pallas kernels  26.4 us (24%)
  starting transfers between devices  2.56 us (2%)
  waiting for transfers between devices  1.92 us (2%)
    all_to_all x1, blocking collectives, shards(): lax.all_to_all(white.reshape(n, FB // n, white.shape[1]), 'tm', split_axi...  44.5 us
    reshape x2, local copies, waits for them, and re-layouts, correlate(): return out.reshape(ROUNDS, bins, 2, tiles * LANES)  19.2 us
    pallas_call x1, Pallas kernels, whiten(): pl.pallas_call(functools.partial(spectra, rows), grid=(steps,), in_specs=...  14.4 us
    pallas_call x1, Pallas kernels, correlate(): pl.pallas_call(functools.partial(pairing, wins, chans, 1.0 / wins), grid=...  12.1 us
    reshape x1, local copies, waits for them, and re-layouts, correlate(): out = out.reshape(ROUNDS, bins, tiles, 2, LANES).transpose(0, 1, 3, 2, 4)  6.59 us
    another operation x6, local copies, waits for them, and re-layouts, shards(): sources = jnp.tile(jnp.stack(got), (1, 1, 1, 1, LANES // SRC))  4.77 us
    unnamed x8, local copies, waits for them, and re-layouts  3.01 us
    ppermute x2, starting transfers between devices, passed_along(): return lax.ppermute(block, axis, route)  2.56 us
  transfers between devices with their start and end apart: 2, of which 2 were waited for; matrix products, arithmetic and copies ran while one was open for 1% of the time, Pallas kernels for 0%

commit v1 on v0

--- a/solution.py
+++ b/solution.py
@@ -238,8 +238,8 @@
                 q = ai[w] * br - ar[w] * bi
                 real = p if real is None else real + p
                 imag = q if imag is None else imag + q
-            o_ref[rnd, pl.ds(2 * tile, KB, stride=2 * tiles), :] = real * scale
-            o_ref[rnd, pl.ds(2 * tile + 1, KB, stride=2 * tiles), :] = imag * scale
+            o_ref[rnd, :, 0, lanes] = real * scale
+            o_ref[rnd, :, 1, lanes] = imag * scale
 
 
 def correlate(grouped, sources):
@@ -256,14 +256,13 @@
             pl.BlockSpec((ROUNDS, wins, 2, KB, LANES), lambda i: (0, 0, 0, i, 0)),
             pl.BlockSpec(spread.shape, lambda i: (0, 0)),
         ],
-        out_specs=pl.BlockSpec((ROUNDS, KB * tiles * 2, LANES), lambda i: (0, i, 0)),
-        out_shape=jax.ShapeDtypeStruct((ROUNDS, bins * tiles * 2, LANES), jnp.float32),
+        out_specs=pl.BlockSpec((ROUNDS, KB, 2, chans * SRC), lambda i: (0, i, 0, 0)),
+        out_shape=jax.ShapeDtypeStruct((ROUNDS, bins, 2, chans * SRC), jnp.float32),
         scratch_shapes=[pltpu.VMEM((2 * wins * KB, chans * SRC), jnp.float32)],
         compiler_params=pltpu.CompilerParams(vmem_limit_bytes=48 << 20),
         name="pairing",
     )(grouped, sources, jnp.asarray(spread))
-    out = out.reshape(ROUNDS, bins, tiles, 2, LANES).transpose(0, 1, 3, 2, 4)
-    return out.reshape(ROUNDS, bins, 2, tiles * LANES)
+    return out
 
 
 def passed_along(block, axis, distance):

time: 111 us -> 86.5 us (0.78)
  local copies, waits for them, and re-layouts: 34 us -> 8.17 us
  Pallas kernels: 26.4 us -> 28.3 us
    reshape x3 -> x0, local copies, waits for them, and re-layouts: 25.8 us -> none  [the longest x2 19.2 us: correlate(): return out.reshape(ROUNDS, bins, 2, tiles * LANES)]
    pallas_call x1, Pallas kernels: 12.1 us -> 13.9 us  [correlate(): pl.pallas_call(functools.partial(pairing, wins, chans, 1.0 / wins), grid=...]
where the time goes in v1:
time: 86.5 us; the launch traced here: 86.2 us
  blocking collectives  44.5 us (51%)
  Pallas kernels  28.3 us (33%)
  local copies, waits for them, and re-layouts  8.17 us (9%)
  starting transfers between devices  2.56 us (3%)
  waiting for transfers between devices  1.92 us (2%)
    all_to_all x1, blocking collectives, shards(): lax.all_to_all(white.reshape(n, FB // n, white.shape[1]), 'tm', split_axi...  44.5 us
    pallas_call x1, Pallas kernels, whiten(): pl.pallas_call(functools.partial(spectra, rows), grid=(steps,), in_specs=...  14.4 us
    pallas_call x1, Pallas kernels, correlate(): pl.pallas_call(functools.partial(pairing, wins, chans, 1.0 / wins), grid=...  13.9 us
    another operation x6, local copies, waits for them, and re-layouts, shards(): sources = jnp.tile(jnp.stack(got), (1, 1, 1, 1, LANES // SRC))  4.77 us
    unnamed x8, local copies, waits for them, and re-layouts  3.01 us
    ppermute x2, starting transfers between devices, passed_along(): return lax.ppermute(block, axis, route)  2.56 us
    ppermute x2, waiting for transfers between devices, passed_along(): return lax.ppermute(block, axis, route)  1.92 us
  transfers between devices with their start and end apart: 2, of which 2 were waited for; matrix products, arithmetic and copies ran while one was open for 1% of the time, Pallas kernels for 0%

profile of v1, /device:TPU:0, one launch (start us, length us, event | category | flops | bytes accessed | tf_op | source)
XLA Modules:
  0.0 86.2 jit_solution(14856871443977356620)
XLA Ops:
  0.7 0.0 copy-start
  0.7 1.1 %copy-done = bf16[640,640]{1,0:T(8,128)(2,1)S(1)} copy-done((bf16[640,640]{1,0:T(8,128)(2,1)S(1)}, bf16[640,640]{1,0:T(8,128)(2,1)}, u32[]{:S(2)}) %copy-start) | copy-done | bytes 819224
  1.8 0.0 copy-start.2
  1.8 0.9 %copy-done.2 = f32[14,8,512]{2,1,0:T(8,128)S(1)} copy-done((f32[14,8,512]{2,1,0:T(8,128)S(1)}, f32[14,8,512]{2,1,0:T(8,128)}, u32[]{:S(2)}) %copy-start.2) | copy-done | bytes 229400
  2.7 0.0 copy-start.3
  2.7 0.9 %copy-done.3 = bf16[192,512]{1,0:T(8,128)(2,1)S(1)} copy-done((bf16[192,512]{1,0:T(8,128)(2,1)S(1)}, bf16[192,512]{1,0:T(8,128)(2,1)}, u32[]{:S(2)}) %copy-start.3) | copy-done | bytes 196632
  3.7 14.4 %whiten.1 = f32[640,640]{1,0:T(8,128)S(1)} custom-call(s32[1]{0:T(128)S(6)} %copy.20.off_ref, f32[19840,128]{1,0:T(8,128)} %bitcast.11, bf16[192,512]{1,0:T(8,128)(2,1)S(1)} %copy-done.3, f32[14,8,512]{2,1,0:T(8,128)S(1)} %copy-done.2, bf16[640,640]{1,0:T(8,128)(2,1)S(1)} %copy-done), custom_call_target="tpu_custom_call" | custom-call | tf_op jit(solution)/shard_map/whiten/pallas_call | solution.py:184
  18.0 44.5 %all_to_all.5.a_ref = f32[4,160,640]{2,1,0:T(8,128)S(1)} all-to-all(f32[4,160,640]{2,1,0:T(8,128)S(1)} %bitcast.10), channel_id=1, replica_groups=mesh['chan'=8,'tm'=4] {'tm'}, dimensions={0} | all-to-all | bytes 3276800 | tf_op jit(solution)/shard_map/all_to_all | solution.py:279
  62.7 0.3 reshape.15
  63.0 1.1 %collective-permute-start = (f32[80,128]{1,0:T(8,128)S(1)}, f32[80,128]{1,0:T(8,128)S(1)}, u32[]{:S(2)}, u32[]{:S(2)}) collective-permute-start(f32[80,128]{1,0:T(8,128)S(1)} %reshape.15), channel_id=1, source_target_pairs={{4,0},{8,4},{12,8},{16,12},{20,16},{24,20},{28,24},{0,28},{5,1},{9... | collective-permute-start | bytes 122888 | tf_op jit(solution)/shard_map/ppermute | solution.py:271
  64.2 1.4 %collective-permute-start.1 = (f32[80,128]{1,0:T(8,128)S(1)}, f32[80,128]{1,0:T(8,128)S(1)}, u32[]{:S(2)}, u32[]{:S(2)}) collective-permute-start(f32[80,128]{1,0:T(8,128)S(1)} %reshape.15), channel_id=1, source_target_pairs={{8,0},{12,4},{16,8},{20,12},{24,16},{28,20},{0,24},{4,28},{9,1},{1... | collective-permute-start | bytes 122888 | tf_op jit(solution)/shard_map/ppermute | solution.py:271
  65.6 0.3 collective-permute-done
  65.8 0.4 stack_reshape.6
  66.2 0.3 copy.17
  66.5 1.7 %collective-permute-done.1 = f32[80,128]{1,0:T(8,128)S(1)} collective-permute-done((f32[80,128]{1,0:T(8,128)S(1)}, f32[80,128]{1,0:T(8,128)S(1)}, u32[]{:S(2)}, u32[]{:S(2)}) %collective-permute-start.1) | collective-permute-done | bytes 40992 | tf_op jit(solution)/shard_map/ppermute | solution.py:271
  68.2 0.4 stack_reshape.7
  68.5 0.3 copy.18
  68.9 1.5 %broadcast_bitcast_fusion = f32[2,4,2,160,128]{3,4,2,1,0:T(8,128)} fusion(f32[2,4,2,160,8]{3,4,2,1,0:T(8,128)S(1)} %pad_maximum_fusion.1), kind=kLoop, calls=%fused_computation | loop fusion | bytes 1392640 | tf_op jit(solution)/shard_map/tile | solution.py:284
  70.3 0.0 copy-start.1
  70.3 2.0 %copy.19.b_ref = f32[2,4,2,160,128]{4,3,2,1,0:T(8,128)S(1)} copy(f32[2,4,2,160,128]{3,4,2,1,0:T(8,128)} %broadcast_bitcast_fusion) | data formatting | bytes 2621440 | tf_op jit(solution)/shard_map/tile | solution.py:284
  72.3 0.0 copy-done.1
  72.3 13.9 %pairing.1 = f32[2,160,2,2560]{3,2,1,0:T(2,128)} custom-call(f32[4,160,640]{2,1,0:T(8,128)S(1)} %all_to_all.5.a_ref, f32[2,4,2,160,128]{4,3,2,1,0:T(8,128)S(1)} %copy.19.b_ref, bf16[256,1024]{1,0:T(8,128)(2,1)S(1)} %copy-done.1), custom_call_target="tpu_custom_call" | custom-call | tf_op jit(solution)/shard_map/pairing/pallas_call | solution.py:251
  (4 shorter events, 0.2 us)
Async XLA Ops:
  0.7 1.1 %copy-start = (bf16[640,640]{1,0:T(8,128)(2,1)S(1)}, bf16[640,640]{1,0:T(8,128)(2,1)}, u32[]{:S(2)}) copy-start(bf16[640,640]{1,0:T(8,128)(2,1)} %constant.10.clone.band_ref) | copy-start | bytes 2457604
  1.8 0.9 %copy-start.2 = (f32[14,8,512]{2,1,0:T(8,128)S(1)}, f32[14,8,512]{2,1,0:T(8,128)}, u32[]{:S(2)}) copy-start(f32[14,8,512]{2,1,0:T(8,128)} %constant.9.clone.twiddle_ref) | copy-start | bytes 688132
  2.7 0.9 %copy-start.3 = (bf16[192,512]{1,0:T(8,128)(2,1)S(1)}, bf16[192,512]{1,0:T(8,128)(2,1)}, u32[]{:S(2)}) copy-start(bf16[192,512]{1,0:T(8,128)(2,1)} %constant.8.clone.both_ref) | copy-start | bytes 589828
  63.0 2.8 %collective-permute-start = (f32[80,128]{1,0:T(8,128)S(1)}, f32[80,128]{1,0:T(8,128)S(1)}, u32[]{:S(2)}, u32[]{:S(2)}) collective-permute-start(f32[80,128]{1,0:T(8,128)S(1)} %reshape.15), channel_id=1, source_target_pairs={{4,0},{8,4},{12,8},{16,12},{20,16},{24,20},{28,24},{0,28},{5,1},{9... | collective-permute-start | bytes 122888 | tf_op jit(solution)/shard_map/ppermute | solution.py:271
  64.2 4.0 %collective-permute-start.1 = (f32[80,128]{1,0:T(8,128)S(1)}, f32[80,128]{1,0:T(8,128)S(1)}, u32[]{:S(2)}, u32[]{:S(2)}) collective-permute-start(f32[80,128]{1,0:T(8,128)S(1)} %reshape.15), channel_id=1, source_target_pairs={{8,0},{12,4},{16,8},{20,12},{24,16},{28,20},{0,24},{4,28},{9,1},{1... | collective-permute-start | bytes 122888 | tf_op jit(solution)/shard_map/ppermute | solution.py:271
  70.3 2.0 %copy-start.1 = (bf16[256,1024]{1,0:T(8,128)(2,1)S(1)}, bf16[256,1024]{1,0:T(8,128)(2,1)}, u32[]{:S(2)}) copy-start(bf16[256,1024]{1,0:T(8,128)(2,1)} %constant.11.clone.e_ref) | copy-start | bytes 1572868
